TPU v7x, 256 devices: a whole 4x4x8 slice. The times are simulated.
256 devices in a mesh: dp: 8 (over x, core), expert: 32 (over z, y).
Axes of the slice: x: 4, y: 4, z: 8, core: 2. Of those that a mesh axis runs over, the one named last changes fastest.
Arguments:
- tokens: bfloat16 [2048, 3584], P(('dp', 'expert')), may hold values from -6 to 6
- cotangent: bfloat16 [2048, 3584], P(('dp', 'expert')), may hold values from -6 to 6
- routes: int32 [2048, 8], P(('dp', 'expert')), may hold values from 0 to 31, all different within a row; in each aligned block of 8 rows (0 to 7, 8 to 15, ...) at most 3 rows name the same one
- gates: bfloat16 [2048, 8], P(('dp', 'expert')), may hold values from 0.049804688 to 1
- w_gate: bfloat16 [32, 3584, 2048], P('expert', None, 'dp'), may hold values from -0.09375 to 0.09375
- w_up: bfloat16 [32, 3584, 2048], P('expert', None, 'dp'), may hold values from -0.09375 to 0.09375
- w_down: bfloat16 [32, 2048, 3584], P('expert', 'dp'), may hold values from -0.125 to 0.125
Outputs:
- grad_tokens: bfloat16 [2048, 3584], P(('dp', 'expert'))
- grad_gate: bfloat16 [32, 3584, 2048], P('expert', None, 'dp')
- grad_up: bfloat16 [32, 3584, 2048], P('expert', None, 'dp')
- grad_down: bfloat16 [32, 2048, 3584], P('expert', 'dp')
Inputs may be any that keep to these rules, and one draw needn't show every extreme that they name: `routes`: each row names 8 different experts; among the rows of one device no expert is named more than 3 times, a bound that some block reaches.
All inputs are finite; a program needn't handle non-finite values.
Results may differ from a plain program's by a relative error of at most 0.01.
Values may be sent and summed in bfloat16 or wider, within the bound.
No kernel may reach another device: no remote copies, remote signals or barrier semaphores. Data moves between devices by JAX's collectives and lax.ppermute only.
A program may use at most 128 MiB of HBM per device.

v0:
```python
import functools

import jax
import jax.numpy as jnp
from jax import lax
from jax.experimental import pallas as pl
from jax.experimental.pallas import tpu as pltpu
from jax.sharding import PartitionSpec as P


BF = jnp.bfloat16
F32 = jnp.float32
LANES = 128
SLOTS = 3


def held(a):
    return pltpu.with_memory_space_constraint(a, pltpu.VMEM)


def chunk_rows(tiles):
    return -(-SLOTS * tiles // 8) * 8


def deal(scratch, experts, tiles, value):
    chunk = chunk_rows(tiles)
    for j in range(SLOTS):
        for c in range(tiles):
            scratch[pl.ds(j * tiles + c, experts, stride=chunk), :] = value(
                slice(j * experts, (j + 1) * experts), slice(c * LANES, (c + 1) * LANES)
            )
    for n in range(SLOTS * tiles, chunk):
        scratch[pl.ds(n, experts, stride=chunk), :] = jnp.zeros((experts, LANES), F32)


def collect(scratch, experts, tiles, out):
    chunk = chunk_rows(tiles)
    for j in range(SLOTS):
        for c in range(tiles):
            out[j * experts : (j + 1) * experts, c * LANES : (c + 1) * LANES] = scratch[
                pl.ds(j * tiles + c, experts, stride=chunk), :
            ].astype(BF)


def pack_kernel(tok, cot, routes, gates, out_x, out_dy, pick, picked, scratch, *, experts):
    rows, features = tok.shape
    top = routes.shape[1]
    tiles = features // LANES
    lane = lax.broadcasted_iota(jnp.int32, (rows, LANES), 1)
    expert_of = lane % experts
    slot_of = lane // experts
    hit = jnp.zeros((rows, LANES), F32)
    gate = jnp.zeros((rows, LANES), F32)
    for k in range(top):
        same = routes[:, k : k + 1] == expert_of
        hit = jnp.where(same, 1.0, hit)
        gate = jnp.where(same, gates[:, k : k + 1].astype(F32), gate)
    below = lax.broadcasted_iota(jnp.int32, (rows, rows), 1) < lax.broadcasted_iota(jnp.int32, (rows, rows), 0)
    rank = jnp.dot(below.astype(BF), hit.astype(BF), preferred_element_type=F32)
    chosen = (hit > 0.5) & (rank == slot_of.astype(F32))
    sel = jnp.where(chosen, 1.0, 0.0)
    pick[...] = sel.astype(BF)

    def spread(mask, values):
        return lax.dot_general(mask.astype(BF), values, (((0,), (0,)), ((), ())), preferred_element_type=F32)

    picked[:, :features] = spread(sel, tok[...])
    deal(scratch, experts, tiles, lambda r, c: picked[r, c])
    out_x[...] = scratch[...].astype(BF)
    picked[:, :features] = spread(sel, cot[...])
    picked[:, features:] = spread(sel * gate, jnp.ones((rows, LANES), BF))
    deal(scratch, experts, tiles + 1, lambda r, c: picked[r, c])
    out_dy[...] = scratch[...].astype(BF)


def pack_rows(tokens, cotangent, routes, gates, experts):
    rows, features = tokens.shape
    tiles = features // LANES
    assert chunk_rows(tiles) == chunk_rows(tiles + 1)
    flat = (experts * chunk_rows(tiles), LANES)
    return pl.pallas_call(
        functools.partial(pack_kernel, experts=experts),
        out_shape=(
            jax.ShapeDtypeStruct(flat, BF),
            jax.ShapeDtypeStruct(flat, BF),
            jax.ShapeDtypeStruct((rows, LANES), BF),
        ),
        scratch_shapes=[pltpu.VMEM((LANES, features + LANES), F32), pltpu.VMEM(flat, F32)],
        name="pack_rows",
    )(tokens, cotangent, routes, gates)


def unpack_kernel(flat, out, scratch, *, experts):
    scratch[...] = flat[...].astype(F32)
    collect(scratch, experts, out.shape[1] // LANES, out)


def unpack_rows(flat, experts, width):
    return pl.pallas_call(
        functools.partial(unpack_kernel, experts=experts),
        out_shape=jax.ShapeDtypeStruct((SLOTS * experts, width), BF),
        scratch_shapes=[pltpu.VMEM(flat.shape, F32)],
        name="unpack_rows",
    )(held(flat))


def back_kernel(own, left_low, left_high, right_low, right_high, out, scratch, *, experts):
    half = own.shape[0] // 2

    def value(r, c):
        low, high = slice(r.start, min(r.stop, half)), slice(max(r.start, half) - half, r.stop - half)
        left, right = (
            jnp.concatenate([p[s, c] for p, s in ((a, low), (b, high)) if s.start < s.stop], axis=0).astype(F32)
            for a, b in ((left_low, left_high), (right_low, right_high))
        )
        return own[r, c].astype(F32) + left + right

    deal(scratch, experts, own.shape[1] // LANES, value)
    out[...] = scratch[...].astype(BF)


def pack_back(own, left_low, left_high, right_low, right_high, experts):
    flat = (experts * chunk_rows(own.shape[1] // LANES), LANES)
    return pl.pallas_call(
        functools.partial(back_kernel, experts=experts),
        out_shape=jax.ShapeDtypeStruct(flat, BF),
        scratch_shapes=[pltpu.VMEM(flat, F32)],
        name="pack_back",
    )(*(held(a) for a in (own, left_low, left_high, right_low, right_high)))


def combine_kernel(flat, pick, out, scratch, rows_ref, *, experts):
    scratch[...] = flat[...].astype(F32)
    collect(scratch, experts, out.shape[1] // LANES, rows_ref)
    out[...] = jnp.dot(pick[:, : SLOTS * experts], rows_ref[...], preferred_element_type=F32).astype(BF)


def combine_rows(flat, pick, experts, features):
    return pl.pallas_call(
        functools.partial(combine_kernel, experts=experts),
        out_shape=jax.ShapeDtypeStruct((pick.shape[0], features), BF),
        scratch_shapes=[pltpu.VMEM(flat.shape, F32), pltpu.VMEM((SLOTS * experts, features), BF)],
        name="combine_rows",
    )(held(flat), pick)


def weight_grads_kernel(*refs, xs, dys):
    refs = list(refs)
    take = lambda n: [refs.pop(0) for _ in range(n)]
    rows_x, rows_dy, hidden, d_gate, d_up = take(xs), take(dys), take(dys), take(dys), take(dys)
    out_gate, out_up, out_down = refs

    def product(a, b):
        a, b = (jnp.concatenate([piece[...] for piece in side], axis=0) for side in (a, b))
        return lax.dot_general(a, b, (((0,), (0,)), ((), ())), preferred_element_type=F32).astype(BF)

    out_gate[0] = product(rows_x, d_gate)
    out_up[0] = product(rows_x, d_up)
    out_down[0] = product(hidden, rows_dy)


def weight_grads(rows_x, rows_dy, terms, features):
    step = 512
    width = terms[0][0].shape[1]
    columns = tuple(zip(*terms))
    operands = [*rows_x, *rows_dy, *columns[0], *columns[1], *columns[2]]
    specs = [pl.BlockSpec((a.shape[0], step), lambda i: (0, i)) for a in (*rows_x, *rows_dy)]
    specs += [pl.BlockSpec(a.shape, lambda i: (0, 0)) for a in operands[len(specs) :]]
    tall = pl.BlockSpec((1, step, width), lambda i: (0, i, 0))
    return pl.pallas_call(
        functools.partial(weight_grads_kernel, xs=len(rows_x), dys=len(rows_dy)),
        grid=(features // step,),
        in_specs=specs,
        out_specs=(tall, tall, pl.BlockSpec((1, width, step), lambda i: (0, 0, i))),
        out_shape=(
            jax.ShapeDtypeStruct((1, features, width), BF),
            jax.ShapeDtypeStruct((1, features, width), BF),
            jax.ShapeDtypeStruct((1, width, features), BF),
        ),
        name="weight_grads",
    )(*operands)


def exchange(flat, experts):
    chunks = flat.reshape(experts, -1, LANES)
    out = lax.all_to_all(chunks, "expert", split_axis=0, concat_axis=0, tiled=True)
    return out.reshape(-1, LANES)


def shift(a, by, size):
    return lax.ppermute(a, "dp", [(i, (i + 2 * by) % size) for i in range(size)])


def swap(a, size):
    return lax.ppermute(a, "dp", [(i, i ^ 1) for i in range(size)])


def after(values, *others):
    return lax.optimization_barrier((tuple(values), others))[0] if others else tuple(values)


def projections(rows, gate_mat, up_mat):
    gate_pre = jnp.dot(rows, gate_mat, preferred_element_type=F32)
    up_pre = jnp.dot(rows, up_mat, preferred_element_type=F32)
    return gate_pre, up_pre


def expert_terms(rows, gate_pre, up_pre, gate_mat, up_mat, down_mat):
    features = gate_mat.shape[0]
    weight = rows[:, features : features + 1].astype(F32)
    sig = jax.nn.sigmoid(gate_pre)
    activated = gate_pre * sig
    hidden = (weight * activated * up_pre).astype(BF)
    returned = weight * jnp.dot(rows[:, :features], down_mat.T, preferred_element_type=F32)
    d_gate = (returned * up_pre * sig * (1.0 + gate_pre * (1.0 - sig))).astype(BF)
    d_up = (returned * activated).astype(BF)
    total = jnp.dot(d_gate, gate_mat.T, preferred_element_type=F32) + jnp.dot(
        d_up, up_mat.T, preferred_element_type=F32
    )
    return total, (hidden, d_gate, d_up)


def per_device(tokens, cotangent, routes, gates, w_gate, w_up, w_down):
    features = tokens.shape[1]
    experts = lax.axis_size("expert")
    size = lax.axis_size("dp")
    mats = w_gate[0], w_up[0], w_down[0]
    flat_x, flat_dy, pick = pack_rows(tokens, cotangent, routes, gates, experts)
    own_x = unpack_rows(exchange(flat_x, experts), experts, features)
    rows = own_x.shape[0]
    half = rows // 2
    behind, ahead = shift(own_x, 1, size), shift(own_x, -1, size)
    halves = behind[:half], ahead[half:]
    far = shift(halves[0], 1, size), shift(halves[1], -1, size)
    (flat_dy,) = after((exchange(flat_dy, experts),), *halves)
    own_dy = unpack_rows(flat_dy, experts, features + LANES)
    near_xm = jnp.concatenate(after((own_x, behind, ahead), own_dy), axis=0)
    near_xt = swap(near_xm, size)
    pre_nm = projections(near_xm, *mats[:2])
    pre_nt = projections(near_xt, *mats[:2])
    far_xm = jnp.concatenate(after(far, *pre_nm), axis=0)
    far_xt = swap(far_xm, size)
    pre_fm = projections(far_xm, *mats[:2])
    pre_ft = projections(far_xt, *mats[:2])
    sides = shift(own_dy, 1, size), shift(own_dy, -1, size)
    behind, ahead = after(sides, *pre_nt, *pre_fm, *pre_ft)
    halves = behind[:half], ahead[half:]
    far = shift(halves[0], 1, size), shift(halves[1], -1, size)
    near_m = jnp.concatenate(after((own_dy, behind, ahead), *halves), axis=0)
    near_t = swap(near_m, size)
    total_nm, terms_nm = expert_terms(near_m, *pre_nm, *mats)
    (near_t,) = after((near_t,), total_nm)
    total_nt, terms_nt = expert_terms(near_t, *pre_nt, *mats)
    swapped = swap(total_nt.astype(BF), size)
    far_m = jnp.concatenate(after(far, total_nt), axis=0)
    total_fm, terms_fm = expert_terms(far_m, *pre_fm, *mats)
    (far_t,) = after((swap(far_m, size),), total_fm)
    total_ft, terms_ft = expert_terms(far_t, *pre_ft, *mats)
    (total_ft,) = after((total_ft.astype(BF),), swapped)
    across = (total_fm + swap(total_ft, size).astype(F32)).astype(BF)
    total_n = total_nm + swapped.astype(F32)
    own, behind, ahead = (total_n[k * rows : (k + 1) * rows] for k in range(3))
    right_ready = shift(behind[:half].astype(BF), -1, size)
    left_ready = shift(ahead[half:].astype(BF), 1, size)
    from_behind = shift(across[:half], 1, size).astype(F32)
    from_ahead = shift(across[half:], -1, size).astype(F32)
    left_late = shift((ahead[:half] + from_behind).astype(BF), 1, size)
    right_late = shift((behind[half:] + from_ahead).astype(BF), -1, size)
    sides = left_late, left_ready, right_ready, right_late
    back = exchange(pack_back(own.astype(BF), *sides, experts), experts)
    grad_x = combine_rows(back, pick, experts, features)
    grads = weight_grads(
        (near_xm, far_xm, near_xt, far_xt), (near_m, far_m, near_t, far_t), (terms_nm, terms_fm, terms_nt, terms_ft), features
    )
    return (grad_x, *grads)


def solution(mesh):
    rows = P(("dp", "expert"), None)
    columns = P("expert", None, "dp")
    down = P("expert", "dp", None)
    return jax.shard_map(
        per_device,
        mesh=mesh,
        in_specs=(rows, rows, rows, rows, columns, columns, down),
        out_specs=(rows, columns, columns, down),
        check_vma=False,
    )
```

profile of v0, /device:TPU:8, one launch (start us, length us, event | category | flops | bytes accessed | tf_op | source)
XLA Modules:
  0.0 173.6 jit_solution(12627892674946807497)
XLA Ops:
  0.6 2.7 %pack_rows.1 = (bf16[2816,128]{1,0:T(8,128)(2,1)}, bf16[2816,128]{1,0:T(8,128)(2,1)}, bf16[8,128]{1,0:T(8,128)(2,1)}) custom-call(bf16[8,3584]{1,0:T(8,128)(2,1)} %tok.1, bf16[8,3584]{1,0:T(8,128)(2,1)} %cot.1, s32[8,8]{1,0:T(8,128)} %routes.1, bf16[8,8]{1,0:T(8,128)(2,1)} %gates.1), custom_call_target="tpu_custom_call" | custom-call | tf_op jit(solution)/shard_map/pack_rows/pallas_call | solution.py:81
  3.3 32.7 %all_to_all.15 = bf16[32,88,128]{2,1,0:T(8,128)(2,1)S(1)} all-to-all(bf16[32,88,128]{2,1,0:T(8,128)(2,1)} %bitcast.86), channel_id=1, replica_groups=mesh['dp'=8,'expert'=32] {'expert'}, dimensions={0} | all-to-all | bytes 1441792 | tf_op jit(solution)/shard_map/all_to_all | solution.py:186
  36.1 5.6 %all-to-all-start = ((bf16[32,88,128]{2,1,0:T(8,128)(2,1)}), bf16[32,88,128]{2,1,0:T(8,128)(2,1)S(1)}, u32[]{:S(2)}, u32[]{:S(2)}) async-start(bf16[32,88,128]{2,1,0:T(8,128)(2,1)} %bitcast.85), calls=%async_computation | async-start | bytes 1441792 | tf_op jit(solution)/shard_map/all_to_all | solution.py:186
  41.7 1.2 unpack_rows.2
  42.9 1.5 collective-permute-start
  44.3 1.7 %collective-permute-start.1 = (bf16[96,3584]{1,0:T(8,128)(2,1)}, bf16[96,3584]{1,0:T(8,128)(2,1)S(1)}, u32[]{:S(2)}, u32[]{:S(2)}) collective-permute-start(bf16[96,3584]{1,0:T(8,128)(2,1)} %unpack_rows.2), channel_id=1, source_target_pairs={{0,192},{32,224},{64,0},{96,32},{128,64},{160,96},{192,128},{224,1... | collective-permute-start | bytes 2064392 | tf_op jit(solution)/shard_map/ppermute | solution.py:191
  46.1 13.7 %collective-permute-done = bf16[96,3584]{1,0:T(8,128)(2,1)S(1)} collective-permute-done((bf16[96,3584]{1,0:T(8,128)(2,1)}, bf16[96,3584]{1,0:T(8,128)(2,1)S(1)}, u32[]{:S(2)}, u32[]{:S(2)}) %collective-permute-start) | collective-permute-done | bytes 688160 | tf_op jit(solution)/shard_map/ppermute | solution.py:191
  60.2 0.8 slice.86
  61.0 3.0 %collective-permute-start.6 = (bf16[48,3584]{1,0:T(8,128)(2,1)}, bf16[48,3584]{1,0:T(8,128)(2,1)}, u32[]{:S(2)}, u32[]{:S(2)}) collective-permute-start(bf16[48,3584]{1,0:T(8,128)(2,1)} %slice.86), channel_id=1, source_target_pairs={{0,192},{32,224},{64,0},{96,32},{128,64},{160,96},{192,128},{224,1... | collective-permute-start | bytes 1032200 | tf_op jit(solution)/shard_map/ppermute | solution.py:191
  63.9 1.2 unpack_rows.3
  65.4 2.0 %copy-done.1 = bf16[1,3584,256]{2,1,0:T(8,128)(2,1)S(1)} copy-done((bf16[1,3584,256]{2,1,0:T(8,128)(2,1)S(1)}, bf16[1,3584,256]{2,1,0:T(8,128)(2,1)}, u32[]{:S(2)}) %copy-start.1) | copy-done | bytes 1835032
  67.4 0.7 fusion.19
  68.1 0.7 fusion.35
  69.0 1.0 constant_dynamic-update-slice_fusion.3.refs_1_
  70.1 1.1 collective-permute-start.2
  71.2 2.8 %collective-permute-start.3 = (bf16[96,3712]{1,0:T(8,128)(2,1)S(1)}, bf16[96,3712]{1,0:T(8,128)(2,1)S(1)}, u32[]{:S(2)}, u32[]{:S(2)}) collective-permute-start(bf16[96,3712]{1,0:T(8,128)(2,1)S(1)} %copy-done.6), channel_id=1, source_target_pairs={{0,192},{32,224},{64,0},{96,32},{128,64},{160,96},{192,128},{224,1... | collective-permute-start | bytes 2138120 | tf_op jit(solution)/shard_map/ppermute | solution.py:191
  75.8 0.7 fusion.37
  77.2 0.7 fusion.21
  77.9 12.6 %collective-permute-done.2 = bf16[96,3712]{1,0:T(8,128)(2,1)S(1)} collective-permute-done((bf16[96,3712]{1,0:T(8,128)(2,1)S(1)}, bf16[96,3712]{1,0:T(8,128)(2,1)S(1)}, u32[]{:S(2)}, u32[]{:S(2)}) %collective-permute-start.2) | collective-permute-done | bytes 712736 | tf_op jit(solution)/shard_map/ppermute | solution.py:191
  91.1 1.2 collective-permute-start.10
  92.3 2.1 %collective-permute-start.11 = (bf16[48,3712]{1,0:T(8,128)(2,1)S(1)}, bf16[48,3712]{1,0:T(8,128)(2,1)S(1)}, u32[]{:S(2)}, u32[]{:S(2)}) collective-permute-start(bf16[48,3712]{1,0:T(8,128)(2,1)S(1)} %slice.69), channel_id=1, source_target_pairs={{0,192},{32,224},{64,0},{96,32},{128,64},{160,96},{192,128},{224,1... | collective-permute-start | bytes 1069064 | tf_op jit(solution)/shard_map/ppermute | solution.py:191
  94.5 1.4 multiply_convert_fusion.1
  95.9 0.7 fusion.29
  96.7 0.8 convolution_add_fusion.1
  97.7 1.4 multiply_convert_fusion
  99.1 0.7 fusion.27
  99.9 0.8 convolution_add_fusion
  100.8 2.2 %collective-permute-done.10 = bf16[48,3712]{1,0:T(8,128)(2,1)S(1)} collective-permute-done((bf16[48,3712]{1,0:T(8,128)(2,1)S(1)}, bf16[48,3712]{1,0:T(8,128)(2,1)S(1)}, u32[]{:S(2)}, u32[]{:S(2)}) %collective-permute-start.10) | collective-permute-done | bytes 356384 | tf_op jit(solution)/shard_map/ppermute | solution.py:191
  103.3 1.2 multiply_convert_fusion.7
  104.5 0.7 fusion.25
  105.2 0.7 convolution_add_fusion.3
  106.1 1.2 multiply_convert_fusion.6
  108.0 0.7 fusion
  109.3 0.7 fusion.63
  110.1 1.0 collective-permute-done.13
  111.3 3.0 %collective-permute-start.18 = (bf16[48,3584]{1,0:T(8,128)(2,1)S(1)}, bf16[48,3584]{1,0:T(8,128)(2,1)S(1)}, u32[]{:S(2)}, u32[]{:S(2)}) collective-permute-start(bf16[48,3584]{1,0:T(8,128)(2,1)S(1)} %get-tuple-element.54), channel_id=1, source_target_pairs={{0,192},{32,224},{64,0},{96,32},{128,64},{160,96},{192,128},{224,1... | collective-permute-start | bytes 1032200 | tf_op jit(solution)/shard_map/ppermute | solution.py:191
  114.3 0.8 collective-permute-start.16
  115.1 2.9 %collective-permute-start.17 = (bf16[48,3584]{1,0:T(8,128)(2,1)S(1)}, bf16[48,3584]{1,0:T(8,128)(2,1)S(1)}, u32[]{:S(2)}, u32[]{:S(2)}) collective-permute-start(bf16[48,3584]{1,0:T(8,128)(2,1)S(1)} %get-tuple-element.52), channel_id=1, source_target_pairs={{0,192},{32,224},{64,0},{96,32},{128,64},{160,96},{192,128},{224,1... | collective-permute-start | bytes 1032200 | tf_op jit(solution)/shard_map/ppermute | solution.py:191
  117.9 4.8 %collective-permute-done.18 = bf16[48,3584]{1,0:T(8,128)(2,1)S(1)} collective-permute-done((bf16[48,3584]{1,0:T(8,128)(2,1)S(1)}, bf16[48,3584]{1,0:T(8,128)(2,1)S(1)}, u32[]{:S(2)}, u32[]{:S(2)}) %collective-permute-start.18) | collective-permute-done | bytes 344096 | tf_op jit(solution)/shard_map/ppermute | solution.py:191
  122.7 3.7 %collective-permute-done.14 = bf16[48,3584]{1,0:T(8,128)(2,1)S(1)} collective-permute-done((bf16[48,3584]{1,0:T(8,128)(2,1)S(1)}, bf16[48,3584]{1,0:T(8,128)(2,1)S(1)}, u32[]{:S(2)}, u32[]{:S(2)}) %collective-permute-start.14) | collective-permute-done | bytes 344096 | tf_op jit(solution)/shard_map/ppermute | solution.py:191
  126.6 3.2 %collective-permute-start.19 = (bf16[48,3584]{1,0:T(8,128)(2,1)S(1)}, bf16[48,3584]{1,0:T(8,128)(2,1)S(1)}, u32[]{:S(2)}, u32[]{:S(2)}) collective-permute-start(bf16[48,3584]{1,0:T(8,128)(2,1)S(1)} %get-tuple-element.50), channel_id=1, source_target_pairs={{0,192},{32,224},{64,0},{96,32},{128,64},{160,96},{192,128},{224,1... | collective-permute-start | bytes 1032200 | tf_op jit(solution)/shard_map/ppermute | solution.py:191
  129.9 3.9 %collective-permute-done.16.left_high = bf16[48,3584]{1,0:T(8,128)(2,1)S(1)} collective-permute-done((bf16[48,3584]{1,0:T(8,128)(2,1)S(1)}, bf16[48,3584]{1,0:T(8,128)(2,1)S(1)}, u32[]{:S(2)}, u32[]{:S(2)}) %collective-permute-start.16) | collective-permute-done | bytes 344096 | tf_op jit(solution)/shard_map/ppermute | solution.py:191
  133.8 6.5 %collective-permute-done.15.left_low = bf16[48,3584]{1,0:T(8,128)(2,1)S(1)} collective-permute-done((bf16[48,3584]{1,0:T(8,128)(2,1)S(1)}, bf16[48,3584]{1,0:T(8,128)(2,1)S(1)}, u32[]{:S(2)}, u32[]{:S(2)}) %collective-permute-start.15) | collective-permute-done | bytes 344096 | tf_op jit(solution)/shard_map/ppermute | solution.py:191
  140.3 1.2 pack_back.1
  141.5 9.8 %all-to-all-start.2 = ((bf16[32,88,128]{2,1,0:T(8,128)(2,1)}), bf16[32,88,128]{2,1,0:T(8,128)(2,1)S(1)}, u32[]{:S(2)}, u32[]{:S(2)}) async-start(bf16[32,88,128]{2,1,0:T(8,128)(2,1)} %bitcast.84), calls=%async_computation.2 | async-start | bytes 1441792 | tf_op jit(solution)/shard_map/all_to_all | solution.py:186
  151.3 10.3 %weight_grads.1 = (bf16[1,3584,256]{2,1,0:T(8,128)(2,1)}, bf16[1,3584,256]{2,1,0:T(8,128)(2,1)}, bf16[1,256,3584]{2,1,0:T(8,128)(2,1)}) custom-call(bf16[288,3584]{1,0:T(8,128)(2,1)} %copy-done.5, bf16[96,3584]{1,0:T(8,128)(2,1)} %copy-done.2, bf16[288,3584]{1,0:T(8,128)(2,1)} %copy-done.9, bf16[96,3584]{1,0:T(8,128)(2,1)} %copy-done.3, ...), custom_call_target="tpu_custom_call" | custom-call | tf_op jit(solution)/shard_map/weight_grads/pallas_call | solution.py:170
  161.6 10.2 %all-to-all-done.2 = bf16[32,88,128]{2,1,0:T(8,128)(2,1)S(1)} async-done(((bf16[32,88,128]{2,1,0:T(8,128)(2,1)}), bf16[32,88,128]{2,1,0:T(8,128)(2,1)S(1)}, u32[]{:S(2)}, u32[]{:S(2)}) %all-to-all-start.2) | async-done | bytes 720928 | tf_op jit(solution)/shard_map/all_to_all | solution.py:186
  171.8 1.8 %combine_rows.1 = bf16[8,3584]{1,0:T(8,128)(2,1)} custom-call(bf16[2816,128]{1,0:T(8,128)(2,1)S(1)} %bitcast.81, bf16[8,128]{1,0:T(8,128)(2,1)} %get-tuple-element.44.pick), custom_call_target="tpu_custom_call" | custom-call | tf_op jit(solution)/shard_map/combine_rows/pallas_call | solution.py:139
  (89 shorter events, 6.3 us)
Async XLA Ops:
  36.1 27.8 %all-to-all-start = ((bf16[32,88,128]{2,1,0:T(8,128)(2,1)}), bf16[32,88,128]{2,1,0:T(8,128)(2,1)S(1)}, u32[]{:S(2)}, u32[]{:S(2)}) async-start(bf16[32,88,128]{2,1,0:T(8,128)(2,1)} %bitcast.85), calls=%async_computation | async-start | bytes 1441792 | tf_op jit(solution)/shard_map/all_to_all | solution.py:186
  42.9 22.3 %copy-start.7 = (bf16[96,3584]{1,0:T(8,128)(2,1)S(1)}, bf16[96,3584]{1,0:T(8,128)(2,1)}, u32[]{:S(2)}) copy-start(bf16[96,3584]{1,0:T(8,128)(2,1)} %unpack_rows.2) | copy-start | bytes 2064388
  42.9 16.9 %collective-permute-start = (bf16[96,3584]{1,0:T(8,128)(2,1)}, bf16[96,3584]{1,0:T(8,128)(2,1)S(1)}, u32[]{:S(2)}, u32[]{:S(2)}) collective-permute-start(bf16[96,3584]{1,0:T(8,128)(2,1)} %unpack_rows.2), channel_id=1, source_target_pairs={{0,64},{32,96},{64,128},{96,160},{128,192},{160,224},{192,0},{224,... | collective-permute-start | bytes 2064392 | tf_op jit(solution)/shard_map/ppermute | solution.py:191
  44.3 15.8 %collective-permute-start.1 = (bf16[96,3584]{1,0:T(8,128)(2,1)}, bf16[96,3584]{1,0:T(8,128)(2,1)S(1)}, u32[]{:S(2)}, u32[]{:S(2)}) collective-permute-start(bf16[96,3584]{1,0:T(8,128)(2,1)} %unpack_rows.2), channel_id=1, source_target_pairs={{0,192},{32,224},{64,0},{96,32},{128,64},{160,96},{192,128},{224,1... | collective-permute-start | bytes 2064392 | tf_op jit(solution)/shard_map/ppermute | solution.py:191
  59.8 9.0 %collective-permute-start.5 = (bf16[48,3584]{1,0:T(8,128)(2,1)S(1)}, bf16[48,3584]{1,0:T(8,128)(2,1)S(1)}, u32[]{:S(2)}, u32[]{:S(2)}) collective-permute-start(bf16[48,3584]{1,0:T(8,128)(2,1)S(1)} %slice.85), channel_id=1, source_target_pairs={{0,64},{32,96},{64,128},{96,160},{128,192},{160,224},{192,0},{224,... | collective-permute-start | bytes 1032200 | tf_op jit(solution)/shard_map/ppermute | solution.py:191
  61.0 8.0 %collective-permute-start.6 = (bf16[48,3584]{1,0:T(8,128)(2,1)}, bf16[48,3584]{1,0:T(8,128)(2,1)}, u32[]{:S(2)}, u32[]{:S(2)}) collective-permute-start(bf16[48,3584]{1,0:T(8,128)(2,1)} %slice.86), channel_id=1, source_target_pairs={{0,192},{32,224},{64,0},{96,32},{128,64},{160,96},{192,128},{224,1... | collective-permute-start | bytes 1032200 | tf_op jit(solution)/shard_map/ppermute | solution.py:191
  65.1 2.2 %copy-start.1 = (bf16[1,3584,256]{2,1,0:T(8,128)(2,1)S(1)}, bf16[1,3584,256]{2,1,0:T(8,128)(2,1)}, u32[]{:S(2)}) copy-start(bf16[1,3584,256]{2,1,0:T(8,128)(2,1)} %param.12) | copy-start | bytes 5505028
  65.3 2.8 %copy-start.5 = (bf16[288,3584]{1,0:T(8,128)(2,1)}, bf16[288,3584]{1,0:T(8,128)(2,1)S(1)}, u32[]{:S(2)}) copy-start(bf16[288,3584]{1,0:T(8,128)(2,1)S(1)} %constant_dynamic-update-slice_fusion.refs_0_) | copy-start | bytes 6193156
  65.3 2.8 %copy-start = (bf16[1,3584,256]{2,1,0:T(8,128)(2,1)S(1)}, bf16[1,3584,256]{2,1,0:T(8,128)(2,1)}, u32[]{:S(2)}) copy-start(bf16[1,3584,256]{2,1,0:T(8,128)(2,1)} %param.11) | copy-start | bytes 5505028
  65.3 10.5 %collective-permute-start.4 = (bf16[288,3584]{1,0:T(8,128)(2,1)S(1)}, bf16[288,3584]{1,0:T(8,128)(2,1)S(1)}, u32[]{:S(2)}, u32[]{:S(2)}) collective-permute-start(bf16[288,3584]{1,0:T(8,128)(2,1)S(1)} %constant_dynamic-update-slice_fusion.refs_0_), channel_id=1, source_target_pairs={{0,32},{32,0},{64,96},{96,64},{128,160},{160,128},{192,224},{224,1... | collective-permute-start | bytes 6193160 | tf_op jit(solution)/shard_map/ppermute | solution.py:195
  68.1 2.0 %copy-start.6 = (bf16[96,3712]{1,0:T(8,128)(2,1)S(1)}, bf16[96,3712]{1,0:T(8,128)(2,1)}, u32[]{:S(2)}) copy-start(bf16[96,3712]{1,0:T(8,128)(2,1)} %unpack_rows.3) | copy-start | bytes 2138116
  70.0 4.8 %copy-start.2 = (bf16[96,3584]{1,0:T(8,128)(2,1)}, bf16[96,3584]{1,0:T(8,128)(2,1)S(1)}, u32[]{:S(2)}) copy-start(bf16[96,3584]{1,0:T(8,128)(2,1)S(1)} %constant_dynamic-update-slice_fusion.3.refs_1_) | copy-start | bytes 2064388
  70.0 4.8 %collective-permute-start.7 = (bf16[96,3584]{1,0:T(8,128)(2,1)S(1)}, bf16[96,3584]{1,0:T(8,128)(2,1)S(1)}, u32[]{:S(2)}, u32[]{:S(2)}) collective-permute-start(bf16[96,3584]{1,0:T(8,128)(2,1)S(1)} %constant_dynamic-update-slice_fusion.3.refs_1_), channel_id=1, source_target_pairs={{0,32},{32,0},{64,96},{96,64},{128,160},{160,128},{192,224},{224,1... | collective-permute-start | bytes 2064392 | tf_op jit(solution)/shard_map/ppermute | solution.py:195
  70.1 20.3 %collective-permute-start.2 = (bf16[96,3712]{1,0:T(8,128)(2,1)S(1)}, bf16[96,3712]{1,0:T(8,128)(2,1)S(1)}, u32[]{:S(2)}, u32[]{:S(2)}) collective-permute-start(bf16[96,3712]{1,0:T(8,128)(2,1)S(1)} %copy-done.6), channel_id=1, source_target_pairs={{0,64},{32,96},{64,128},{96,160},{128,192},{160,224},{192,0},{224,... | collective-permute-start | bytes 2138120 | tf_op jit(solution)/shard_map/ppermute | solution.py:191
  71.2 19.2 %collective-permute-start.3 = (bf16[96,3712]{1,0:T(8,128)(2,1)S(1)}, bf16[96,3712]{1,0:T(8,128)(2,1)S(1)}, u32[]{:S(2)}, u32[]{:S(2)}) collective-permute-start(bf16[96,3712]{1,0:T(8,128)(2,1)S(1)} %copy-done.6), channel_id=1, source_target_pairs={{0,192},{32,224},{64,0},{96,32},{128,64},{160,96},{192,128},{224,1... | collective-permute-start | bytes 2138120 | tf_op jit(solution)/shard_map/ppermute | solution.py:191
  74.9 0.9 copy-start.3
  75.8 1.4 copy-start.9
  90.5 4.0 %copy-start.20 = (bf16[1,256,3584]{2,1,0:T(8,128)(2,1)S(1)}, bf16[1,256,3584]{2,1,0:T(8,128)(2,1)}, u32[]{:S(2)}) copy-start(bf16[1,256,3584]{2,1,0:T(8,128)(2,1)} %param.13) | copy-start | bytes 5505028
  90.8 5.2 %copy-start.4 = (bf16[288,3712]{1,0:T(8,128)(2,1)}, bf16[288,3712]{1,0:T(8,128)(2,1)S(1)}, u32[]{:S(2)}) copy-start(bf16[288,3712]{1,0:T(8,128)(2,1)S(1)} %constant_dynamic-update-slice_fusion.5.refs_4_) | copy-start | bytes 6414340
  90.8 6.8 %collective-permute-start.8 = (bf16[288,3712]{1,0:T(8,128)(2,1)S(1)}, bf16[288,3712]{1,0:T(8,128)(2,1)S(1)}, u32[]{:S(2)}, u32[]{:S(2)}) collective-permute-start(bf16[288,3712]{1,0:T(8,128)(2,1)S(1)} %constant_dynamic-update-slice_fusion.5.refs_4_), channel_id=1, source_target_pairs={{0,32},{32,0},{64,96},{96,64},{128,160},{160,128},{192,224},{224,1... | collective-permute-start | bytes 6414344 | tf_op jit(solution)/shard_map/ppermute | solution.py:195
  91.1 11.9 %collective-permute-start.10 = (bf16[48,3712]{1,0:T(8,128)(2,1)S(1)}, bf16[48,3712]{1,0:T(8,128)(2,1)S(1)}, u32[]{:S(2)}, u32[]{:S(2)}) collective-permute-start(bf16[48,3712]{1,0:T(8,128)(2,1)S(1)} %slice.68), channel_id=1, source_target_pairs={{0,64},{32,96},{64,128},{96,160},{128,192},{160,224},{192,0},{224,... | collective-permute-start | bytes 1069064 | tf_op jit(solution)/shard_map/ppermute | solution.py:191
  92.3 10.7 %collective-permute-start.11 = (bf16[48,3712]{1,0:T(8,128)(2,1)S(1)}, bf16[48,3712]{1,0:T(8,128)(2,1)S(1)}, u32[]{:S(2)}, u32[]{:S(2)}) collective-permute-start(bf16[48,3712]{1,0:T(8,128)(2,1)S(1)} %slice.69), channel_id=1, source_target_pairs={{0,192},{32,224},{64,0},{96,32},{128,64},{160,96},{192,128},{224,1... | collective-permute-start | bytes 1069064 | tf_op jit(solution)/shard_map/ppermute | solution.py:191
  95.9 0.7 copy-start.12
  95.9 0.8 copy-start.11
  97.5 1.6 copy-start.8
  99.1 0.7 copy-start.13
  99.1 0.8 copy-start.15
  100.7 8.0 %collective-permute-start.9 = (bf16[288,3584]{1,0:T(8,128)(2,1)S(1)}, bf16[288,3584]{1,0:T(8,128)(2,1)S(1)}, u32[]{:S(2)}, u32[]{:S(2)}) collective-permute-start(bf16[288,3584]{1,0:T(8,128)(2,1)S(1)} %convolution_add_fusion), channel_id=1, source_target_pairs={{0,32},{32,0},{64,96},{96,64},{128,160},{160,128},{192,224},{224,1... | collective-permute-start | bytes 6193160 | tf_op jit(solution)/shard_map/ppermute | solution.py:195
  103.1 2.1 %copy-start.10 = (bf16[96,3712]{1,0:T(8,128)(2,1)}, bf16[96,3712]{1,0:T(8,128)(2,1)S(1)}, u32[]{:S(2)}) copy-start(bf16[96,3712]{1,0:T(8,128)(2,1)S(1)} %constant_dynamic-update-slice_fusion.8.refs_5_) | copy-start | bytes 2138116
  103.1 2.9 %collective-permute-start.12 = (bf16[96,3712]{1,0:T(8,128)(2,1)S(1)}, bf16[96,3712]{1,0:T(8,128)(2,1)S(1)}, u32[]{:S(2)}, u32[]{:S(2)}) collective-permute-start(bf16[96,3712]{1,0:T(8,128)(2,1)S(1)} %constant_dynamic-update-slice_fusion.8.refs_5_), channel_id=1, source_target_pairs={{0,32},{32,0},{64,96},{96,64},{128,160},{160,128},{192,224},{224,1... | collective-permute-start | bytes 2138120 | tf_op jit(solution)/shard_map/ppermute | solution.py:195
  104.5 1.4 copy-start.16
  104.5 1.4 copy-start.18
  105.9 2.0 %copy-start.14 = (bf16[96,3712]{1,0:T(8,128)(2,1)}, bf16[96,3712]{1,0:T(8,128)(2,1)S(1)}, u32[]{:S(2)}) copy-start(bf16[96,3712]{1,0:T(8,128)(2,1)S(1)} %collective-permute-done.12.refs_7_) | copy-start | bytes 2138116
  107.3 1.4 copy-start.17
  107.3 1.4 copy-start.19
  108.7 2.4 %collective-permute-start.13 = (bf16[96,3584]{1,0:T(8,128)(2,1)S(1)}, bf16[96,3584]{1,0:T(8,128)(2,1)S(1)}, u32[]{:S(2)}, u32[]{:S(2)}) collective-permute-start(bf16[96,3584]{1,0:T(8,128)(2,1)S(1)} %fusion), channel_id=1, source_target_pairs={{0,32},{32,0},{64,96},{96,64},{128,160},{160,128},{192,224},{224,1... | collective-permute-start | bytes 2064392 | tf_op jit(solution)/shard_map/ppermute | solution.py:195
  111.3 11.5 %collective-permute-start.18 = (bf16[48,3584]{1,0:T(8,128)(2,1)S(1)}, bf16[48,3584]{1,0:T(8,128)(2,1)S(1)}, u32[]{:S(2)}, u32[]{:S(2)}) collective-permute-start(bf16[48,3584]{1,0:T(8,128)(2,1)S(1)} %get-tuple-element.54), channel_id=1, source_target_pairs={{0,192},{32,224},{64,0},{96,32},{128,64},{160,96},{192,128},{224,1... | collective-permute-start | bytes 1032200 | tf_op jit(solution)/shard_map/ppermute | solution.py:191
  114.3 12.1 %collective-permute-start.14 = (bf16[48,3584]{1,0:T(8,128)(2,1)S(1)}, bf16[48,3584]{1,0:T(8,128)(2,1)S(1)}, u32[]{:S(2)}, u32[]{:S(2)}) collective-permute-start(bf16[48,3584]{1,0:T(8,128)(2,1)S(1)} %get-tuple-element.55), channel_id=1, source_target_pairs={{0,64},{32,96},{64,128},{96,160},{128,192},{160,224},{192,0},{224,... | collective-permute-start | bytes 1032200 | tf_op jit(solution)/shard_map/ppermute | solution.py:191
  114.3 19.5 %collective-permute-start.16 = (bf16[48,3584]{1,0:T(8,128)(2,1)S(1)}, bf16[48,3584]{1,0:T(8,128)(2,1)S(1)}, u32[]{:S(2)}, u32[]{:S(2)}) collective-permute-start(bf16[48,3584]{1,0:T(8,128)(2,1)S(1)} %get-tuple-element.53), channel_id=1, source_target_pairs={{0,64},{32,96},{64,128},{96,160},{128,192},{160,224},{192,0},{224,... | collective-permute-start | bytes 1032200 | tf_op jit(solution)/shard_map/ppermute | solution.py:191
  115.1 18.7 %collective-permute-start.17 = (bf16[48,3584]{1,0:T(8,128)(2,1)S(1)}, bf16[48,3584]{1,0:T(8,128)(2,1)S(1)}, u32[]{:S(2)}, u32[]{:S(2)}) collective-permute-start(bf16[48,3584]{1,0:T(8,128)(2,1)S(1)} %get-tuple-element.52), channel_id=1, source_target_pairs={{0,192},{32,224},{64,0},{96,32},{128,64},{160,96},{192,128},{224,1... | collective-permute-start | bytes 1032200 | tf_op jit(solution)/shard_map/ppermute | solution.py:191
  126.5 13.8 %collective-permute-start.15 = (bf16[48,3584]{1,0:T(8,128)(2,1)S(1)}, bf16[48,3584]{1,0:T(8,128)(2,1)S(1)}, u32[]{:S(2)}, u32[]{:S(2)}) collective-permute-start(bf16[48,3584]{1,0:T(8,128)(2,1)S(1)} %get-tuple-element.51), channel_id=1, source_target_pairs={{0,64},{32,96},{64,128},{96,160},{128,192},{160,224},{192,0},{224,... | collective-permute-start | bytes 1032200 | tf_op jit(solution)/shard_map/ppermute | solution.py:191
  126.6 13.7 %collective-permute-start.19 = (bf16[48,3584]{1,0:T(8,128)(2,1)S(1)}, bf16[48,3584]{1,0:T(8,128)(2,1)S(1)}, u32[]{:S(2)}, u32[]{:S(2)}) collective-permute-start(bf16[48,3584]{1,0:T(8,128)(2,1)S(1)} %get-tuple-element.50), channel_id=1, source_target_pairs={{0,192},{32,224},{64,0},{96,32},{128,64},{160,96},{192,128},{224,1... | collective-permute-start | bytes 1032200 | tf_op jit(solution)/shard_map/ppermute | solution.py:191
  141.5 30.2 %all-to-all-start.2 = ((bf16[32,88,128]{2,1,0:T(8,128)(2,1)}), bf16[32,88,128]{2,1,0:T(8,128)(2,1)S(1)}, u32[]{:S(2)}, u32[]{:S(2)}) async-start(bf16[32,88,128]{2,1,0:T(8,128)(2,1)} %bitcast.84), calls=%async_computation.2 | async-start | bytes 1441792 | tf_op jit(solution)/shard_map/all_to_all | solution.py:186
where the time goes:
time: 174 us
  waiting for transfers between devices  58.7 us (34%)
  starting transfers between devices  40.2 us (23%)
  blocking collectives  32.7 us (19%)
  Pallas kernels  18.5 us (11%)
  matrix products  15.7 us (9%)
  local copies, waits for them, and re-layouts  5.12 us (3%)
    ppermute x14, waiting for transfers between devices, shift(): lax.ppermute(a, 'dp', [(i, (i + 2 * by) % size) for i in range(size)])  47.5 us
    all_to_all x1, blocking collectives, exchange(): lax.all_to_all(chunks, 'expert', split_axis=0, concat_axis=0, tiled=True)  32.7 us
    ppermute x14, starting transfers between devices, shift(): lax.ppermute(a, 'dp', [(i, (i + 2 * by) % size) for i in range(size)])  23.7 us
    all_to_all x2, starting transfers between devices, exchange(): lax.all_to_all(chunks, 'expert', split_axis=0, concat_axis=0, tiled=True)  15.3 us
    pallas_call x1, Pallas kernels, weight_grads(): pl.pallas_call(functools.partial(weight_grads_kernel, xs=len(rows_x), dys...  10.3 us
    all_to_all x2, waiting for transfers between devices, exchange(): lax.all_to_all(chunks, 'expert', split_axis=0, concat_axis=0, tiled=True)  10.2 us
    dot_general x4, matrix products, expert_terms(): jnp.dot(rows[:, :features], down_mat.T, preferred_element_type=F32)  5.38 us
  transfers between devices with their start and end apart: 22, of which 10 were waited for; matrix products, arithmetic and copies ran while one was open for 11% of the time, Pallas kernels for 7%

commit v1 on v0

--- a/solution.py
+++ b/solution.py
@@ -234,43 +234,52 @@
     far = shift(halves[0], 1, size), shift(halves[1], -1, size)
     (flat_dy,) = after((exchange(flat_dy, experts),), *halves)
     own_dy = unpack_rows(flat_dy, experts, features + LANES)
-    near_xm = jnp.concatenate(after((own_x, behind, ahead), own_dy), axis=0)
+    early = shift(own_dy[:half], 1, size), shift(own_dy[half:], -1, size)
+    near_xm = jnp.concatenate(after((own_x, *halves, behind[half:], ahead[:half]), own_dy), axis=0)
     near_xt = swap(near_xm, size)
     pre_nm = projections(near_xm, *mats[:2])
+    far_xm = jnp.concatenate(after(far, *pre_nm), axis=0)
+    far_x = jnp.concatenate((far_xm, swap(far_xm, size)), axis=0)
+    early = after(early, far_x)
+    far = shift(early[0], 1, size), shift(early[1], -1, size)
     pre_nt = projections(near_xt, *mats[:2])
-    far_xm = jnp.concatenate(after(far, *pre_nm), axis=0)
-    far_xt = swap(far_xm, size)
-    pre_fm = projections(far_xm, *mats[:2])
-    pre_ft = projections(far_xt, *mats[:2])
-    sides = shift(own_dy, 1, size), shift(own_dy, -1, size)
-    behind, ahead = after(sides, *pre_nt, *pre_fm, *pre_ft)
-    halves = behind[:half], ahead[half:]
-    far = shift(halves[0], 1, size), shift(halves[1], -1, size)
-    near_m = jnp.concatenate(after((own_dy, behind, ahead), *halves), axis=0)
-    near_t = swap(near_m, size)
-    total_nm, terms_nm = expert_terms(near_m, *pre_nm, *mats)
-    (near_t,) = after((near_t,), total_nm)
-    total_nt, terms_nt = expert_terms(near_t, *pre_nt, *mats)
-    swapped = swap(total_nt.astype(BF), size)
-    far_m = jnp.concatenate(after(far, total_nt), axis=0)
-    total_fm, terms_fm = expert_terms(far_m, *pre_fm, *mats)
-    (far_t,) = after((swap(far_m, size),), total_fm)
-    total_ft, terms_ft = expert_terms(far_t, *pre_ft, *mats)
-    (total_ft,) = after((total_ft.astype(BF),), swapped)
-    across = (total_fm + swap(total_ft, size).astype(F32)).astype(BF)
-    total_n = total_nm + swapped.astype(F32)
-    own, behind, ahead = (total_n[k * rows : (k + 1) * rows] for k in range(3))
-    right_ready = shift(behind[:half].astype(BF), -1, size)
-    left_ready = shift(ahead[half:].astype(BF), 1, size)
+    pre_f = projections(far_x, *mats[:2])
+    soon = 2 * rows
+    early_m = jnp.concatenate(after((own_dy, *early), *pre_nt, *pre_f), axis=0)
+    early_t = swap(early_m, size)
+    late = after((own_dy[half:], own_dy[:half]), early_t)
+    late = shift(late[0], 1, size), shift(late[1], -1, size)
+    total_et, terms_et = expert_terms(early_t, *(a[:soon] for a in pre_nt), *mats)
+    total_et = total_et.astype(BF)
+    total_em, terms_em = expert_terms(*after((early_m,), total_et), *(a[:soon] for a in pre_nm), *mats)
+    total_e = total_em + swap(total_et, size).astype(F32)
+    far_m = jnp.concatenate(after(far, total_em), axis=0)
+    far_t = swap(far_m, size)
+    own = total_e[:rows]
+    right_ready = shift(total_e[rows : rows + half].astype(BF), -1, size)
+    left_ready = shift(total_e[rows + half :].astype(BF), 1, size)
+    far_dy = jnp.concatenate((far_m, far_t), axis=0)
+    total_f, terms_f = expert_terms(far_dy, *pre_f, *mats)
+    across = (total_f[:rows] + swap(total_f[rows:].astype(BF), size).astype(F32)).astype(BF)
     from_behind = shift(across[:half], 1, size).astype(F32)
     from_ahead = shift(across[half:], -1, size).astype(F32)
-    left_late = shift((ahead[:half] + from_behind).astype(BF), 1, size)
-    right_late = shift((behind[half:] + from_ahead).astype(BF), -1, size)
+    late_m = jnp.concatenate(after(late, total_f), axis=0)
+    late_t = swap(late_m, size)
+    late_dy = jnp.concatenate(after((late_m, late_t), across), axis=0)
+    pre_l = (jnp.concatenate((m[soon:], t[soon:]), axis=0) for m, t in zip(pre_nm, pre_nt))
+    total_l, terms_l = expert_terms(late_dy, *pre_l, *mats)
+    total_l = total_l[:rows] + swap(total_l[rows:].astype(BF), size).astype(F32)
+    right_late = shift((total_l[:half] + from_ahead).astype(BF), -1, size)
+    left_late = shift((total_l[half:] + from_behind).astype(BF), 1, size)
     sides = left_late, left_ready, right_ready, right_late
     back = exchange(pack_back(own.astype(BF), *sides, experts), experts)
     grad_x = combine_rows(back, pick, experts, features)
+    terms_lm, terms_lt = tuple(a[:rows] for a in terms_l), tuple(a[rows:] for a in terms_l)
     grads = weight_grads(
-        (near_xm, far_xm, near_xt, far_xt), (near_m, far_m, near_t, far_t), (terms_nm, terms_fm, terms_nt, terms_ft), features
+        (near_xm, near_xt, far_x),
+        (early_m, late_m, early_t, late_t, far_dy),
+        (terms_em, terms_lm, terms_et, terms_lt, terms_f),
+        features,
     )
     return (grad_x, *grads)
 

time: 174 us -> 169 us (0.971)
  the two profiles are of different devices: /device:TPU:8 before, /device:TPU:6 now
where the time goes in v1:
time: 169 us; the launch traced here: 168 us
  waiting for transfers between devices  59.4 us (35%)
  blocking collectives  33.1 us (20%)
  starting transfers between devices  32.6 us (19%)
  Pallas kernels  18.4 us (11%)
  matrix products  14.7 us (9%)
  local copies, waits for them, and re-layouts  7.66 us (5%)
    ppermute x16, waiting for transfers between devices, shift(): lax.ppermute(a, 'dp', [(i, (i + 2 * by) % size) for i in range(size)])  42.7 us
    all_to_all x1, blocking collectives, exchange(): lax.all_to_all(chunks, 'expert', split_axis=0, concat_axis=0, tiled=True)  33.1 us
    ppermute x16, starting transfers between devices, shift(): lax.ppermute(a, 'dp', [(i, (i + 2 * by) % size) for i in range(size)])  17.9 us
    all_to_all x2, starting transfers between devices, exchange(): lax.all_to_all(chunks, 'expert', split_axis=0, concat_axis=0, tiled=True)  13.1 us
    all_to_all x2, waiting for transfers between devices, exchange(): lax.all_to_all(chunks, 'expert', split_axis=0, concat_axis=0, tiled=True)  11.2 us
    pallas_call x1, Pallas kernels, weight_grads(): pl.pallas_call(functools.partial(weight_grads_kernel, xs=len(rows_x), dys...  10.3 us
    ppermute x8, waiting for transfers between devices, swap(): return lax.ppermute(a, 'dp', [(i, i ^ 1) for i in range(size)])  5.48 us
    dot_general x4, matrix products, expert_terms(): jnp.dot(rows[:, :features], down_mat.T, preferred_element_type=F32)  4.84 us
  transfers between devices with their start and end apart: 26, of which 16 were waited for; matrix products, arithmetic and copies ran while one was open for 11% of the time, Pallas kernels for 7%

profile of v1, /device:TPU:6, one launch (start us, length us, event | category | flops | bytes accessed | tf_op | source)
XLA Modules:
  0.0 168.4 jit_solution(16428174793878531763)
XLA Ops:
  0.6 2.7 %pack_rows.1 = (bf16[2816,128]{1,0:T(8,128)(2,1)}, bf16[2816,128]{1,0:T(8,128)(2,1)}, bf16[8,128]{1,0:T(8,128)(2,1)}) custom-call(bf16[8,3584]{1,0:T(8,128)(2,1)} %tok.1, bf16[8,3584]{1,0:T(8,128)(2,1)} %cot.1, s32[8,8]{1,0:T(8,128)} %routes.1, bf16[8,8]{1,0:T(8,128)(2,1)} %gates.1), custom_call_target="tpu_custom_call" | custom-call | tf_op jit(solution)/shard_map/pack_rows/pallas_call | solution.py:81
  3.3 33.1 %all_to_all.15 = bf16[32,88,128]{2,1,0:T(8,128)(2,1)S(1)} all-to-all(bf16[32,88,128]{2,1,0:T(8,128)(2,1)} %bitcast.79), channel_id=1, replica_groups=mesh['dp'=8,'expert'=32] {'expert'}, dimensions={0} | all-to-all | bytes 1441792 | tf_op jit(solution)/shard_map/all_to_all | solution.py:186
  36.5 1.2 unpack_rows.2
  38.1 5.0 %all-to-all-start = ((bf16[32,88,128]{2,1,0:T(8,128)(2,1)}), bf16[32,88,128]{2,1,0:T(8,128)(2,1)S(1)}, u32[]{:S(2)}, u32[]{:S(2)}) async-start(bf16[32,88,128]{2,1,0:T(8,128)(2,1)} %bitcast), calls=%async_computation | async-start | bytes 1441792 | tf_op jit(solution)/shard_map/all_to_all | solution.py:186
  43.1 1.6 collective-permute-start.1
  44.7 8.6 %collective-permute-done = bf16[96,3584]{1,0:T(8,128)(2,1)S(1)} collective-permute-done((bf16[96,3584]{1,0:T(8,128)(2,1)}, bf16[96,3584]{1,0:T(8,128)(2,1)S(1)}, u32[]{:S(2)}, u32[]{:S(2)}) %collective-permute-start) | collective-permute-done | bytes 688160 | tf_op jit(solution)/shard_map/ppermute | solution.py:191
  53.4 1.6 collective-permute-start.4
  54.9 5.2 %collective-permute-done.1 = bf16[96,3584]{1,0:T(8,128)(2,1)S(1)} collective-permute-done((bf16[96,3584]{1,0:T(8,128)(2,1)}, bf16[96,3584]{1,0:T(8,128)(2,1)S(1)}, u32[]{:S(2)}, u32[]{:S(2)}) %collective-permute-start.1) | collective-permute-done | bytes 688160 | tf_op jit(solution)/shard_map/ppermute | solution.py:191
  60.6 2.8 %all-to-all-done = bf16[32,88,128]{2,1,0:T(8,128)(2,1)S(1)} async-done(((bf16[32,88,128]{2,1,0:T(8,128)(2,1)}), bf16[32,88,128]{2,1,0:T(8,128)(2,1)S(1)}, u32[]{:S(2)}, u32[]{:S(2)}) %all-to-all-start) | async-done | bytes 720928 | tf_op jit(solution)/shard_map/all_to_all | solution.py:186
  63.4 1.2 unpack_rows.3
  64.6 1.1 fusion.65
  66.1 1.9 %copy-done = bf16[1,3584,256]{2,1,0:T(8,128)(2,1)S(1)} copy-done((bf16[1,3584,256]{2,1,0:T(8,128)(2,1)S(1)}, bf16[1,3584,256]{2,1,0:T(8,128)(2,1)}, u32[]{:S(2)}) %copy-start) | copy-done | bytes 1835032
  68.8 1.6 collective-permute-start.2
  70.9 0.7 fusion.31
  71.8 2.1 %collective-permute-done.6 = bf16[96,3584]{1,0:T(8,128)(2,1)S(1)} collective-permute-done((bf16[96,3584]{1,0:T(8,128)(2,1)S(1)}, bf16[96,3584]{1,0:T(8,128)(2,1)S(1)}, u32[]{:S(2)}, u32[]{:S(2)}) %collective-permute-start.6) | collective-permute-done | bytes 688160 | tf_op jit(solution)/shard_map/ppermute | solution.py:195
  73.9 3.7 %collective-permute-done.2 = bf16[48,3712]{1,0:T(8,128)(2,1)S(1)} collective-permute-done((bf16[48,3712]{1,0:T(8,128)(2,1)S(1)}, bf16[48,3712]{1,0:T(8,128)(2,1)S(1)}, u32[]{:S(2)}, u32[]{:S(2)}) %collective-permute-start.2) | collective-permute-done | bytes 356384 | tf_op jit(solution)/shard_map/ppermute | solution.py:191
  77.6 2.4 %collective-permute-done.3 = bf16[48,3712]{1,0:T(8,128)(2,1)S(1)} collective-permute-done((bf16[48,3712]{1,0:T(8,128)(2,1)S(1)}, bf16[48,3712]{1,0:T(8,128)(2,1)S(1)}, u32[]{:S(2)}, u32[]{:S(2)}) %collective-permute-start.3) | collective-permute-done | bytes 356384 | tf_op jit(solution)/shard_map/ppermute | solution.py:191
  81.1 0.7 fusion.29
  82.5 0.7 fusion.15
  84.5 1.7 %collective-permute-start.13 = (bf16[48,3712]{1,0:T(8,128)(2,1)S(1)}, bf16[48,3712]{1,0:T(8,128)(2,1)S(1)}, u32[]{:S(2)}, u32[]{:S(2)}) collective-permute-start(bf16[48,3712]{1,0:T(8,128)(2,1)S(1)} %collective-permute-done.3), channel_id=1, source_target_pairs={{0,192},{32,224},{64,0},{96,32},{128,64},{160,96},{192,128},{224,1... | collective-permute-start | bytes 1069064 | tf_op jit(solution)/shard_map/ppermute | solution.py:191
  86.2 1.1 collective-permute-done.8.refs_5_
  87.5 1.4 multiply_convert_fusion.1
  88.8 0.8 fusion.25
  89.6 0.8 fusion
  90.7 1.4 multiply_convert_fusion.3
  92.1 0.8 fusion.23
  93.2 1.7 %collective-permute-start.11 = (bf16[48,3712]{1,0:T(8,128)(2,1)S(1)}, bf16[48,3712]{1,0:T(8,128)(2,1)S(1)}, u32[]{:S(2)}, u32[]{:S(2)}) collective-permute-start(bf16[48,3712]{1,0:T(8,128)(2,1)S(1)} %get-tuple-element.49), channel_id=1, source_target_pairs={{0,192},{32,224},{64,0},{96,32},{128,64},{160,96},{192,128},{224,1... | collective-permute-start | bytes 1069064 | tf_op jit(solution)/shard_map/ppermute | solution.py:191
  95.0 0.8 convolution_add_fusion.2
  96.3 2.1 %collective-permute-done.14 = bf16[96,3712]{1,0:T(8,128)(2,1)S(1)} collective-permute-done((bf16[96,3712]{1,0:T(8,128)(2,1)S(1)}, bf16[96,3712]{1,0:T(8,128)(2,1)S(1)}, u32[]{:S(2)}, u32[]{:S(2)}) %collective-permute-start.14) | collective-permute-done | bytes 712736 | tf_op jit(solution)/shard_map/ppermute | solution.py:195
  98.6 1.4 multiply_convert_fusion
  100.0 0.8 fusion.21
  100.8 0.8 convolution_add_fusion.1
  101.6 1.9 %collective-permute-done.10 = bf16[48,3712]{1,0:T(8,128)(2,1)S(1)} collective-permute-done((bf16[48,3712]{1,0:T(8,128)(2,1)S(1)}, bf16[48,3712]{1,0:T(8,128)(2,1)S(1)}, u32[]{:S(2)}, u32[]{:S(2)}) %collective-permute-start.10) | collective-permute-done | bytes 356384 | tf_op jit(solution)/shard_map/ppermute | solution.py:191
  103.5 1.3 collective-permute-done.11
  106.2 1.7 %collective-permute-start.21 = (bf16[48,3584]{1,0:T(8,128)(2,1)S(1)}, bf16[48,3584]{1,0:T(8,128)(2,1)S(1)}, u32[]{:S(2)}, u32[]{:S(2)}) collective-permute-start(bf16[48,3584]{1,0:T(8,128)(2,1)S(1)} %get-tuple-element.62), channel_id=1, source_target_pairs={{0,192},{32,224},{64,0},{96,32},{128,64},{160,96},{192,128},{224,1... | collective-permute-start | bytes 1032200 | tf_op jit(solution)/shard_map/ppermute | solution.py:191
  109.7 0.8 multiply_convert_fusion.2
  110.4 0.8 fusion.19
  111.2 0.8 convolution_add_fusion
  112.8 2.8 %collective-permute-start.18 = (bf16[48,3584]{1,0:T(8,128)(2,1)S(1)}, bf16[48,3584]{1,0:T(8,128)(2,1)S(1)}, u32[]{:S(2)}, u32[]{:S(2)}) collective-permute-start(bf16[48,3584]{1,0:T(8,128)(2,1)S(1)} %get-tuple-element.67), channel_id=1, source_target_pairs={{0,64},{32,96},{64,128},{96,160},{128,192},{160,224},{192,0},{224,... | collective-permute-start | bytes 1032200 | tf_op jit(solution)/shard_map/ppermute | solution.py:191
  115.8 9.2 %collective-permute-done.22 = bf16[48,3584]{1,0:T(8,128)(2,1)S(1)} collective-permute-done((bf16[48,3584]{1,0:T(8,128)(2,1)S(1)}, bf16[48,3584]{1,0:T(8,128)(2,1)S(1)}, u32[]{:S(2)}, u32[]{:S(2)}) %collective-permute-start.22) | collective-permute-done | bytes 344096 | tf_op jit(solution)/shard_map/ppermute | solution.py:191
  125.1 2.1 %collective-permute-start.19 = (bf16[48,3584]{1,0:T(8,128)(2,1)S(1)}, bf16[48,3584]{1,0:T(8,128)(2,1)S(1)}, u32[]{:S(2)}, u32[]{:S(2)}) collective-permute-start(bf16[48,3584]{1,0:T(8,128)(2,1)S(1)} %get-tuple-element.61), channel_id=1, source_target_pairs={{0,64},{32,96},{64,128},{96,160},{128,192},{160,224},{192,0},{224,... | collective-permute-start | bytes 1032200 | tf_op jit(solution)/shard_map/ppermute | solution.py:191
  127.3 7.1 %collective-permute-done.19.left_low = bf16[48,3584]{1,0:T(8,128)(2,1)S(1)} collective-permute-done((bf16[48,3584]{1,0:T(8,128)(2,1)S(1)}, bf16[48,3584]{1,0:T(8,128)(2,1)S(1)}, u32[]{:S(2)}, u32[]{:S(2)}) %collective-permute-start.19) | collective-permute-done | bytes 344096 | tf_op jit(solution)/shard_map/ppermute | solution.py:191
  134.4 2.9 %collective-permute-done.23.right_high = bf16[48,3584]{1,0:T(8,128)(2,1)S(1)} collective-permute-done((bf16[48,3584]{1,0:T(8,128)(2,1)S(1)}, bf16[48,3584]{1,0:T(8,128)(2,1)S(1)}, u32[]{:S(2)}, u32[]{:S(2)}) %collective-permute-start.23) | collective-permute-done | bytes 344096 | tf_op jit(solution)/shard_map/ppermute | solution.py:191
  137.3 1.2 pack_back.1
  138.5 8.1 %all-to-all-start.2 = ((bf16[32,88,128]{2,1,0:T(8,128)(2,1)}), bf16[32,88,128]{2,1,0:T(8,128)(2,1)S(1)}, u32[]{:S(2)}, u32[]{:S(2)}) async-start(bf16[32,88,128]{2,1,0:T(8,128)(2,1)} %bitcast.78), calls=%async_computation.2 | async-start | bytes 1441792 | tf_op jit(solution)/shard_map/all_to_all | solution.py:186
  147.9 10.3 %weight_grads.1 = (bf16[1,3584,256]{2,1,0:T(8,128)(2,1)}, bf16[1,3584,256]{2,1,0:T(8,128)(2,1)}, bf16[1,256,3584]{2,1,0:T(8,128)(2,1)}) custom-call(bf16[288,3584]{1,0:T(8,128)(2,1)} %copy-done.5, bf16[288,3584]{1,0:T(8,128)(2,1)} %copy-done.10, bf16[192,3584]{1,0:T(8,128)(2,1)} %copy-done.2, bf16[192,3712]{1,0:T(8,128)(2,1)} %copy-done.6, ...), custom_call_target="tpu_custom_call" | custom-call | tf_op jit(solution)/shard_map/weight_grads/pallas_call | solution.py:170
  158.2 8.4 %all-to-all-done.2 = bf16[32,88,128]{2,1,0:T(8,128)(2,1)S(1)} async-done(((bf16[32,88,128]{2,1,0:T(8,128)(2,1)}), bf16[32,88,128]{2,1,0:T(8,128)(2,1)S(1)}, u32[]{:S(2)}, u32[]{:S(2)}) %all-to-all-start.2) | async-done | bytes 720928 | tf_op jit(solution)/shard_map/all_to_all | solution.py:186
  166.6 1.8 %combine_rows.1 = bf16[8,3584]{1,0:T(8,128)(2,1)} custom-call(bf16[2816,128]{1,0:T(8,128)(2,1)S(1)} %bitcast.75, bf16[8,128]{1,0:T(8,128)(2,1)} %get-tuple-element.56.pick), custom_call_target="tpu_custom_call" | custom-call | tf_op jit(solution)/shard_map/combine_rows/pallas_call | solution.py:139
  (121 shorter events, 12.7 us)
Async XLA Ops:
  37.7 15.7 %collective-permute-start = (bf16[96,3584]{1,0:T(8,128)(2,1)}, bf16[96,3584]{1,0:T(8,128)(2,1)S(1)}, u32[]{:S(2)}, u32[]{:S(2)}) collective-permute-start(bf16[96,3584]{1,0:T(8,128)(2,1)} %unpack_rows.2), channel_id=1, source_target_pairs={{0,64},{32,96},{64,128},{96,160},{128,192},{160,224},{192,0},{224,... | collective-permute-start | bytes 2064392 | tf_op jit(solution)/shard_map/ppermute | solution.py:191
  38.1 25.3 %all-to-all-start = ((bf16[32,88,128]{2,1,0:T(8,128)(2,1)}), bf16[32,88,128]{2,1,0:T(8,128)(2,1)S(1)}, u32[]{:S(2)}, u32[]{:S(2)}) async-start(bf16[32,88,128]{2,1,0:T(8,128)(2,1)} %bitcast), calls=%async_computation | async-start | bytes 1441792 | tf_op jit(solution)/shard_map/all_to_all | solution.py:186
  43.1 17.0 %collective-permute-start.1 = (bf16[96,3584]{1,0:T(8,128)(2,1)}, bf16[96,3584]{1,0:T(8,128)(2,1)S(1)}, u32[]{:S(2)}, u32[]{:S(2)}) collective-permute-start(bf16[96,3584]{1,0:T(8,128)(2,1)} %unpack_rows.2), channel_id=1, source_target_pairs={{0,192},{32,224},{64,0},{96,32},{128,64},{160,96},{192,128},{224,1... | collective-permute-start | bytes 2064392 | tf_op jit(solution)/shard_map/ppermute | solution.py:191
  53.4 12.4 %copy-start.8 = (bf16[96,3584]{1,0:T(8,128)(2,1)S(1)}, bf16[96,3584]{1,0:T(8,128)(2,1)}, u32[]{:S(2)}) copy-start(bf16[96,3584]{1,0:T(8,128)(2,1)} %unpack_rows.2) | copy-start | bytes 2064388
  53.4 18.2 %collective-permute-start.4 = (bf16[48,3584]{1,0:T(8,128)(2,1)S(1)}, bf16[48,3584]{1,0:T(8,128)(2,1)S(1)}, u32[]{:S(2)}, u32[]{:S(2)}) collective-permute-start(bf16[48,3584]{1,0:T(8,128)(2,1)S(1)} %get-tuple-element.36), channel_id=1, source_target_pairs={{0,64},{32,96},{64,128},{96,160},{128,192},{160,224},{192,0},{224,... | collective-permute-start | bytes 1032200 | tf_op jit(solution)/shard_map/ppermute | solution.py:191
  60.2 11.4 %collective-permute-start.5 = (bf16[48,3584]{1,0:T(8,128)(2,1)S(1)}, bf16[48,3584]{1,0:T(8,128)(2,1)S(1)}, u32[]{:S(2)}, u32[]{:S(2)}) collective-permute-start(bf16[48,3584]{1,0:T(8,128)(2,1)S(1)} %get-tuple-element.37), channel_id=1, source_target_pairs={{0,192},{32,224},{64,0},{96,32},{128,64},{160,96},{192,128},{224,1... | collective-permute-start | bytes 1032200 | tf_op jit(solution)/shard_map/ppermute | solution.py:191
  65.8 2.2 %copy-start = (bf16[1,3584,256]{2,1,0:T(8,128)(2,1)S(1)}, bf16[1,3584,256]{2,1,0:T(8,128)(2,1)}, u32[]{:S(2)}) copy-start(bf16[1,3584,256]{2,1,0:T(8,128)(2,1)} %param.12) | copy-start | bytes 5505028
  66.0 4.9 %copy-start.5 = (bf16[288,3584]{1,0:T(8,128)(2,1)}, bf16[288,3584]{1,0:T(8,128)(2,1)S(1)}, u32[]{:S(2)}) copy-start(bf16[288,3584]{1,0:T(8,128)(2,1)S(1)} %constant_dynamic-update-slice_fusion.refs_0_) | copy-start | bytes 6193156
  66.0 4.9 %copy-start.1 = (bf16[1,3584,256]{2,1,0:T(8,128)(2,1)S(1)}, bf16[1,3584,256]{2,1,0:T(8,128)(2,1)}, u32[]{:S(2)}) copy-start(bf16[1,3584,256]{2,1,0:T(8,128)(2,1)} %param.11) | copy-start | bytes 5505028
  66.0 15.1 %collective-permute-start.7 = (bf16[288,3584]{1,0:T(8,128)(2,1)S(1)}, bf16[288,3584]{1,0:T(8,128)(2,1)S(1)}, u32[]{:S(2)}, u32[]{:S(2)}) collective-permute-start(bf16[288,3584]{1,0:T(8,128)(2,1)S(1)} %constant_dynamic-update-slice_fusion.refs_0_), channel_id=1, source_target_pairs={{0,32},{32,0},{64,96},{96,64},{128,160},{160,128},{192,224},{224,1... | collective-permute-start | bytes 6193160 | tf_op jit(solution)/shard_map/ppermute | solution.py:195
  68.7 22.0 %copy-start.18 = (f32[288,256]{1,0:T(8,128)}, f32[288,256]{1,0:T(8,128)S(1)}, u32[]{:S(2)}) copy-start(f32[288,256]{1,0:T(8,128)S(1)} %fusion.17) | copy-start | bytes 884740
  68.8 8.9 %collective-permute-start.2 = (bf16[48,3712]{1,0:T(8,128)(2,1)S(1)}, bf16[48,3712]{1,0:T(8,128)(2,1)S(1)}, u32[]{:S(2)}, u32[]{:S(2)}) collective-permute-start(bf16[48,3712]{1,0:T(8,128)(2,1)S(1)} %get-tuple-element.49), channel_id=1, source_target_pairs={{0,64},{32,96},{64,128},{96,160},{128,192},{160,224},{192,0},{224,... | collective-permute-start | bytes 1069064 | tf_op jit(solution)/shard_map/ppermute | solution.py:191
  70.3 9.7 %collective-permute-start.3 = (bf16[48,3712]{1,0:T(8,128)(2,1)S(1)}, bf16[48,3712]{1,0:T(8,128)(2,1)S(1)}, u32[]{:S(2)}, u32[]{:S(2)}) collective-permute-start(bf16[48,3712]{1,0:T(8,128)(2,1)S(1)} %get-tuple-element.48), channel_id=1, source_target_pairs={{0,192},{32,224},{64,0},{96,32},{128,64},{160,96},{192,128},{224,1... | collective-permute-start | bytes 1069064 | tf_op jit(solution)/shard_map/ppermute | solution.py:191
  71.6 19.2 %copy-start.19 = (f32[288,256]{1,0:T(8,128)}, f32[288,256]{1,0:T(8,128)S(1)}, u32[]{:S(2)}) copy-start(f32[288,256]{1,0:T(8,128)S(1)} %fusion.31) | copy-start | bytes 884740
  71.6 2.2 %collective-permute-start.6 = (bf16[96,3584]{1,0:T(8,128)(2,1)S(1)}, bf16[96,3584]{1,0:T(8,128)(2,1)S(1)}, u32[]{:S(2)}, u32[]{:S(2)}) collective-permute-start(bf16[96,3584]{1,0:T(8,128)(2,1)S(1)} %pad_maximum_fusion.1), channel_id=1, source_target_pairs={{0,32},{32,0},{64,96},{96,64},{128,160},{160,128},{192,224},{224,1... | collective-permute-start | bytes 2064392 | tf_op jit(solution)/shard_map/ppermute | solution.py:195
  73.9 6.7 %copy-start.2 = (bf16[192,3584]{1,0:T(8,128)(2,1)}, bf16[192,3584]{1,0:T(8,128)(2,1)S(1)}, u32[]{:S(2)}) copy-start(bf16[192,3584]{1,0:T(8,128)(2,1)S(1)} %constant_dynamic-update-slice_fusion.5.refs_2_) | copy-start | bytes 4128772
  81.1 1.4 copy-start.10
  82.5 4.9 %copy-start.21 = (f32[288,256]{1,0:T(8,128)}, f32[288,256]{1,0:T(8,128)S(1)}, u32[]{:S(2)}) copy-start(f32[288,256]{1,0:T(8,128)S(1)} %fusion.29) | copy-start | bytes 884740
  82.5 1.2 copy-start.3
  83.7 3.7 %copy-start.20 = (f32[288,256]{1,0:T(8,128)}, f32[288,256]{1,0:T(8,128)S(1)}, u32[]{:S(2)}) copy-start(f32[288,256]{1,0:T(8,128)S(1)} %fusion.15) | copy-start | bytes 884740
  83.7 3.7 %copy-start.22 = (bf16[1,256,3584]{2,1,0:T(8,128)(2,1)S(1)}, bf16[1,256,3584]{2,1,0:T(8,128)(2,1)}, u32[]{:S(2)}) copy-start(bf16[1,256,3584]{2,1,0:T(8,128)(2,1)} %param.13) | copy-start | bytes 5505028
  83.8 6.9 %copy-start.6 = (bf16[192,3712]{1,0:T(8,128)(2,1)}, bf16[192,3712]{1,0:T(8,128)(2,1)S(1)}, u32[]{:S(2)}) copy-start(bf16[192,3712]{1,0:T(8,128)(2,1)S(1)} %constant_dynamic-update-slice_fusion.8.refs_3_) | copy-start | bytes 4276228
  83.9 3.5 %collective-permute-start.8 = (bf16[192,3712]{1,0:T(8,128)(2,1)S(1)}, bf16[192,3712]{1,0:T(8,128)(2,1)S(1)}, u32[]{:S(2)}, u32[]{:S(2)}) collective-permute-start(bf16[192,3712]{1,0:T(8,128)(2,1)S(1)} %constant_dynamic-update-slice_fusion.8.refs_3_), channel_id=1, source_target_pairs={{0,32},{32,0},{64,96},{96,64},{128,160},{160,128},{192,224},{224,1... | collective-permute-start | bytes 4276232 | tf_op jit(solution)/shard_map/ppermute | solution.py:195
  84.1 11.6 %collective-permute-start.12 = (bf16[48,3712]{1,0:T(8,128)(2,1)S(1)}, bf16[48,3712]{1,0:T(8,128)(2,1)S(1)}, u32[]{:S(2)}, u32[]{:S(2)}) collective-permute-start(bf16[48,3712]{1,0:T(8,128)(2,1)S(1)} %collective-permute-done.2), channel_id=1, source_target_pairs={{0,64},{32,96},{64,128},{96,160},{128,192},{160,224},{192,0},{224,... | collective-permute-start | bytes 1069064 | tf_op jit(solution)/shard_map/ppermute | solution.py:191
  84.5 11.6 %collective-permute-start.13 = (bf16[48,3712]{1,0:T(8,128)(2,1)S(1)}, bf16[48,3712]{1,0:T(8,128)(2,1)S(1)}, u32[]{:S(2)}, u32[]{:S(2)}) collective-permute-start(bf16[48,3712]{1,0:T(8,128)(2,1)S(1)} %collective-permute-done.3), channel_id=1, source_target_pairs={{0,192},{32,224},{64,0},{96,32},{128,64},{160,96},{192,128},{224,1... | collective-permute-start | bytes 1069064 | tf_op jit(solution)/shard_map/ppermute | solution.py:191
  87.3 1.5 copy-start.11
  90.4 15.2 %collective-permute-start.9 = (bf16[192,3584]{1,0:T(8,128)(2,1)S(1)}, bf16[192,3584]{1,0:T(8,128)(2,1)S(1)}, u32[]{:S(2)}, u32[]{:S(2)}) collective-permute-start(bf16[192,3584]{1,0:T(8,128)(2,1)S(1)} %fusion), channel_id=1, source_target_pairs={{0,32},{32,0},{64,96},{96,64},{128,160},{160,128},{192,224},{224,1... | collective-permute-start | bytes 4128776 | tf_op jit(solution)/shard_map/ppermute | solution.py:195
  92.1 2.9 %copy-start.12 = (bf16[192,256]{1,0:T(8,128)(2,1)}, bf16[192,256]{1,0:T(8,128)(2,1)S(1)}, u32[]{:S(2)}) copy-start(bf16[192,256]{1,0:T(8,128)(2,1)S(1)} %get-tuple-element.76.refs_18_) | copy-start | bytes 294916
  92.9 10.7 %collective-permute-start.10 = (bf16[48,3712]{1,0:T(8,128)(2,1)S(1)}, bf16[48,3712]{1,0:T(8,128)(2,1)S(1)}, u32[]{:S(2)}, u32[]{:S(2)}) collective-permute-start(bf16[48,3712]{1,0:T(8,128)(2,1)S(1)} %get-tuple-element.48), channel_id=1, source_target_pairs={{0,64},{32,96},{64,128},{96,160},{128,192},{160,224},{192,0},{224,... | collective-permute-start | bytes 1069064 | tf_op jit(solution)/shard_map/ppermute | solution.py:191
  93.2 11.7 %collective-permute-start.11 = (bf16[48,3712]{1,0:T(8,128)(2,1)S(1)}, bf16[48,3712]{1,0:T(8,128)(2,1)S(1)}, u32[]{:S(2)}, u32[]{:S(2)}) collective-permute-start(bf16[48,3712]{1,0:T(8,128)(2,1)S(1)} %get-tuple-element.49), channel_id=1, source_target_pairs={{0,192},{32,224},{64,0},{96,32},{128,64},{160,96},{192,128},{224,1... | collective-permute-start | bytes 1069064 | tf_op jit(solution)/shard_map/ppermute | solution.py:191
  96.1 2.3 %collective-permute-start.14 = (bf16[96,3712]{1,0:T(8,128)(2,1)S(1)}, bf16[96,3712]{1,0:T(8,128)(2,1)S(1)}, u32[]{:S(2)}, u32[]{:S(2)}) collective-permute-start(bf16[96,3712]{1,0:T(8,128)(2,1)S(1)} %pad_maximum_fusion), channel_id=1, source_target_pairs={{0,32},{32,0},{64,96},{96,64},{128,160},{160,128},{192,224},{224,1... | collective-permute-start | bytes 2138120 | tf_op jit(solution)/shard_map/ppermute | solution.py:195
  98.5 1.5 copy-start.9
  105.0 3.5 %copy-start.4 = (bf16[96,3712]{1,0:T(8,128)(2,1)}, bf16[96,3712]{1,0:T(8,128)(2,1)S(1)}, u32[]{:S(2)}) copy-start(bf16[96,3712]{1,0:T(8,128)(2,1)S(1)} %constant_dynamic-update-slice_fusion.14.refs_4_) | copy-start | bytes 2138116
  105.0 3.5 %collective-permute-start.15 = (bf16[96,3712]{1,0:T(8,128)(2,1)S(1)}, bf16[96,3712]{1,0:T(8,128)(2,1)S(1)}, u32[]{:S(2)}, u32[]{:S(2)}) collective-permute-start(bf16[96,3712]{1,0:T(8,128)(2,1)S(1)} %constant_dynamic-update-slice_fusion.14.refs_4_), channel_id=1, source_target_pairs={{0,32},{32,0},{64,96},{96,64},{128,160},{160,128},{192,224},{224,1... | collective-permute-start | bytes 2138120 | tf_op jit(solution)/shard_map/ppermute | solution.py:195
  105.1 3.2 %collective-permute-start.16 = (bf16[96,3584]{1,0:T(8,128)(2,1)S(1)}, bf16[96,3584]{1,0:T(8,128)(2,1)S(1)}, u32[]{:S(2)}, u32[]{:S(2)}) collective-permute-start(bf16[96,3584]{1,0:T(8,128)(2,1)S(1)} %slice.249), channel_id=1, source_target_pairs={{0,32},{32,0},{64,96},{96,64},{128,160},{160,128},{192,224},{224,1... | collective-permute-start | bytes 2064392 | tf_op jit(solution)/shard_map/ppermute | solution.py:195
  105.9 21.4 %collective-permute-start.20 = (bf16[48,3584]{1,0:T(8,128)(2,1)S(1)}, bf16[48,3584]{1,0:T(8,128)(2,1)S(1)}, u32[]{:S(2)}, u32[]{:S(2)}) collective-permute-start(bf16[48,3584]{1,0:T(8,128)(2,1)S(1)} %get-tuple-element.63), channel_id=1, source_target_pairs={{0,64},{32,96},{64,128},{96,160},{128,192},{160,224},{192,0},{224,... | collective-permute-start | bytes 1032200 | tf_op jit(solution)/shard_map/ppermute | solution.py:191
  106.2 21.0 %collective-permute-start.21 = (bf16[48,3584]{1,0:T(8,128)(2,1)S(1)}, bf16[48,3584]{1,0:T(8,128)(2,1)S(1)}, u32[]{:S(2)}, u32[]{:S(2)}) collective-permute-start(bf16[48,3584]{1,0:T(8,128)(2,1)S(1)} %get-tuple-element.62), channel_id=1, source_target_pairs={{0,192},{32,224},{64,0},{96,32},{128,64},{160,96},{192,128},{224,1... | collective-permute-start | bytes 1032200 | tf_op jit(solution)/shard_map/ppermute | solution.py:191
  108.4 0.9 slice-start
  108.4 1.0 slice-start.1
  108.4 1.1 slice-start.2
  108.4 1.3 slice-start.3
  108.4 2.0 %copy-start.7 = (bf16[96,3712]{1,0:T(8,128)(2,1)}, bf16[96,3712]{1,0:T(8,128)(2,1)S(1)}, u32[]{:S(2)}) copy-start(bf16[96,3712]{1,0:T(8,128)(2,1)S(1)} %collective-permute-done.15.refs_6_) | copy-start | bytes 2138116
  112.0 3.6 %collective-permute-start.17 = (bf16[96,3584]{1,0:T(8,128)(2,1)S(1)}, bf16[96,3584]{1,0:T(8,128)(2,1)S(1)}, u32[]{:S(2)}, u32[]{:S(2)}) collective-permute-start(bf16[96,3584]{1,0:T(8,128)(2,1)S(1)} %slice.248), channel_id=1, source_target_pairs={{0,32},{32,0},{64,96},{96,64},{128,160},{160,128},{192,224},{224,1... | collective-permute-start | bytes 2064392 | tf_op jit(solution)/shard_map/ppermute | solution.py:195
  112.3 12.6 %collective-permute-start.22 = (bf16[48,3584]{1,0:T(8,128)(2,1)S(1)}, bf16[48,3584]{1,0:T(8,128)(2,1)S(1)}, u32[]{:S(2)}, u32[]{:S(2)}) collective-permute-start(bf16[48,3584]{1,0:T(8,128)(2,1)S(1)} %get-tuple-element.66), channel_id=1, source_target_pairs={{0,192},{32,224},{64,0},{96,32},{128,64},{160,96},{192,128},{224,1... | collective-permute-start | bytes 1032200 | tf_op jit(solution)/shard_map/ppermute | solution.py:191
  112.8 12.1 %collective-permute-start.18 = (bf16[48,3584]{1,0:T(8,128)(2,1)S(1)}, bf16[48,3584]{1,0:T(8,128)(2,1)S(1)}, u32[]{:S(2)}, u32[]{:S(2)}) collective-permute-start(bf16[48,3584]{1,0:T(8,128)(2,1)S(1)} %get-tuple-element.67), channel_id=1, source_target_pairs={{0,64},{32,96},{64,128},{96,160},{128,192},{160,224},{192,0},{224,... | collective-permute-start | bytes 1032200 | tf_op jit(solution)/shard_map/ppermute | solution.py:191
  125.1 9.3 %collective-permute-start.19 = (bf16[48,3584]{1,0:T(8,128)(2,1)S(1)}, bf16[48,3584]{1,0:T(8,128)(2,1)S(1)}, u32[]{:S(2)}, u32[]{:S(2)}) collective-permute-start(bf16[48,3584]{1,0:T(8,128)(2,1)S(1)} %get-tuple-element.61), channel_id=1, source_target_pairs={{0,64},{32,96},{64,128},{96,160},{128,192},{160,224},{192,0},{224,... | collective-permute-start | bytes 1032200 | tf_op jit(solution)/shard_map/ppermute | solution.py:191
  127.1 10.1 %collective-permute-start.23 = (bf16[48,3584]{1,0:T(8,128)(2,1)S(1)}, bf16[48,3584]{1,0:T(8,128)(2,1)S(1)}, u32[]{:S(2)}, u32[]{:S(2)}) collective-permute-start(bf16[48,3584]{1,0:T(8,128)(2,1)S(1)} %get-tuple-element.60), channel_id=1, source_target_pairs={{0,192},{32,224},{64,0},{96,32},{128,64},{160,96},{192,128},{224,1... | collective-permute-start | bytes 1032200 | tf_op jit(solution)/shard_map/ppermute | solution.py:191
  138.5 28.1 %all-to-all-start.2 = ((bf16[32,88,128]{2,1,0:T(8,128)(2,1)}), bf16[32,88,128]{2,1,0:T(8,128)(2,1)S(1)}, u32[]{:S(2)}, u32[]{:S(2)}) async-start(bf16[32,88,128]{2,1,0:T(8,128)(2,1)} %bitcast.78), calls=%async_computation.2 | async-start | bytes 1441792 | tf_op jit(solution)/shard_map/all_to_all | solution.py:186
  (5 other events, 3.8 us)
